TPU v7x, 128 devices: a whole 4x4x4 slice. The times are simulated.
128 devices in a mesh: pb: 4 (over y), ka: 32 (over z, x, core).
Axes of the slice: x: 4, y: 4, z: 4, core: 2. Of those that a mesh axis runs over, the one named last changes fastest.
Arguments:
- envelopes: bfloat16 [256, 147456], P('ka'), may hold values from -6 to 6
- coupling: bfloat16 [8, 9, 32, 9216], P('pb', None, None, 'ka'), may hold values from -3 to 3
- kq_map: int32 [8, 9216], P('pb', 'ka'), may hold values from 0 to 9215, as said below
Outputs:
- exciton_coupling: float32 [8, 9, 256, 256], P('pb', None, 'ka')
Inputs may be any that keep to these rules, and one draw needn't show every extreme that they name: `kq_map`: each row q is a lattice translation: k = kx * 96 + ky goes to ((kx + a_q) mod 96) * 96 + (ky + b_q) mod 96, with -3 <= a_q <= 3; a_q = 3 and a_q = -3 both occur.
All inputs are finite; a program needn't handle non-finite values.
Results may differ from a plain program's by a relative error of at most 0.0029.
Values may be sent and summed in bfloat16 or wider, within the bound.
A program may use at most 64 MiB of HBM per device.

v0:
```python
import math

import jax
import jax.numpy as jnp
from jax import lax
from jax.sharding import PartitionSpec as P

NU = 9
KY = 96


def extended(cells, sides, width):
    for axis, dim in sides:
        count = lax.axis_size(axis)
        head = lax.slice_in_dim(cells, 0, width, axis=dim)
        tail = lax.slice_in_dim(cells, cells.shape[dim] - width, cells.shape[dim], axis=dim)
        cells = jnp.concatenate(
            [
                lax.ppermute(tail, axis, [(i, (i + 1) % count) for i in range(count)]),
                cells,
                lax.ppermute(head, axis, [((i + 1) % count, i) for i in range(count)]),
            ],
            axis=dim,
        )
    return cells


def shards(envelopes, coupling, kq_map):
    n_ka = lax.axis_size("ka")
    s_loc, width = envelopes.shape
    states = s_loc * n_ka
    total_k = width // 16
    lines = total_k // (n_ka * KY)
    lines_all = lines * n_ka
    local_k = lines * KY
    blocks = envelopes.reshape(s_loc, n_ka, local_k * 16)
    mine = lax.all_to_all(blocks, "ka", split_axis=1, concat_axis=0, tiled=True)
    mine = mine.reshape(states, lines, KY * 16)
    padded = extended(mine, (("ka", 1),), lines)
    padded = padded.reshape(states, 3 * local_k, 16)
    own = padded[:, local_k : 2 * local_k].reshape(states, local_k, 4, 4)
    first_line = lax.axis_index("ka") * lines
    line_x = kq_map // KY
    line_y = kq_map % KY
    padded_row = (line_x - first_line + lines) % lines_all
    local_index = padded_row * KY + line_y
    n_q = kq_map.shape[0]
    shifted_all = jnp.stack(
        [
            jnp.take(padded, local_index[qidx], axis=1).reshape(states, local_k * 16)
            for qidx in range(n_q)
        ],
        axis=1,
    )
    factor = 1.0 / math.sqrt(16.0 * lines_all * KY)

    def make_diff(qidx, mode):
        table = coupling[qidx, mode]
        g_cond = table[:16].reshape(4, 4, local_k)
        g_val = table[16:].reshape(4, 4, local_k)
        elec = jnp.einsum("dck,skvc->skvd", g_cond, own, preferred_element_type=jnp.float32)
        hole = jnp.einsum("vwk,skvc->skwc", g_val, own, preferred_element_type=jnp.float32)
        return (elec - hole).astype(jnp.bfloat16).reshape(states, local_k * 16)

    pieces = []
    for qidx in range(n_q):
        left_rows = shifted_all[:, qidx]

        def per_mode(mode):
            diff = make_diff(qidx, mode)
            return jnp.einsum("ap,bp->ab", left_rows, diff, preferred_element_type=jnp.float32)

        partial_sum = lax.map(per_mode, jnp.arange(NU, dtype=jnp.int32))
        pieces.append(lax.psum_scatter(partial_sum, "ka", scatter_dimension=1, tiled=True))
    result = jnp.stack(pieces, axis=0)
    return result * factor


def solution(mesh):
    return jax.shard_map(
        shards,
        mesh=mesh,
        in_specs=(P("ka", None), P("pb", None, None, "ka"), P("pb", "ka")),
        out_specs=P("pb", None, "ka", None),
        check_vma=False,
    )
```

profile of v0, /device:TPU:1, one launch (start us, length us, event | category | flops | bytes accessed | tf_op | source)
XLA Modules:
  0.0 648.5 jit_solution(127613264258414140)
XLA Ops:
  6.5 40.8 %all_to_all.15 = bf16[8,32,4608]{2,0,1:T(8,128)(2,1)S(1)} all-to-all(bf16[8,32,4608]{2,0,1:T(8,128)(2,1)} %bitcast.117), channel_id=1, replica_groups=mesh['pb'=4,'ka'=32] {'ka'}, dimensions={1} | all-to-all | bytes 4718592 | tf_op jit(solution)/shard_map/all_to_all | solution.py:37
  54.5 25.5 %collective-permute-done = bf16[256,3,1536]{2,0,1:T(8,128)(2,1)} collective-permute-done((bf16[256,3,1536]{2,0,1:T(8,128)(2,1)S(1)}, bf16[256,3,1536]{2,0,1:T(8,128)(2,1)}, u32[]{:S(2)}, u32[]{:S(2)}) %collective-permute-start) | collective-permute-done | bytes 2359328 | tf_op jit(solution)/shard_map/ppermute | solution.py:19
  87.5 9.8 %pad_maximum_fusion = bf16[256,9,1536]{2,1,0:T(8,128)(2,1)} fusion(bf16[256,3,1536]{2,1,0:T(4,128)(2,1)S(1)} %copy.39, bf16[256,3,1536]{2,1,0:T(4,128)(2,1)S(1)} %copy-done, bf16[256,3,1536]{2,1,0:T(4,128)(2,1)S(1)} %copy.38), kind=kLoop, calls=%fused_computation.18 | loop fusion | flops 21233664 | bytes 14155776 | tf_op jit(solution)/shard_map/concatenate | solution.py:17
  97.3 16.1 %copy.40 = bf16[256,9,1536]{0,2,1:T(8,128)(2,1)} copy(bf16[256,9,1536]{2,1,0:T(8,128)(2,1)} %pad_maximum_fusion) | data formatting | bytes 14155776 | tf_op jit(solution)/shard_map/concatenate | solution.py:17
  131.5 206.4 %while.20 = (s32[]{:T(128)}, f32[9,256,256]{2,1,0:T(8,128)}, s32[9]{0:T(128)S(1)}, bf16[2,9,32,288]{3,2,1,0:T(8,128)(2,1)}, bf16[256,288,4,4]{0,2,3,1:T(4,128)(2...) while((s32[]{:T(128)}, f32[9,256,256]{2,1,0:T(8,128)}, ...), condition=%wide.region_1.3_spmd, body=%wide.region_0.2_spmd.sunk | while | flops 625213440 | bytes 27392680 | solution.py:73
  139.0 6.4 fusion.47
  145.4 5.0 reshape.84
  162.0 6.4 fusion.47
  168.3 5.0 reshape.84
  184.9 6.4 fusion.47
  191.3 5.0 reshape.84
  207.8 6.4 fusion.47
  230.7 6.4 fusion.47
  253.7 6.4 fusion.47
  276.6 6.4 fusion.47
  299.6 6.4 fusion.47
  322.5 6.4 fusion.47
  338.3 5.6 gather_fusion.1
  353.2 206.6 %while.21 = (s32[]{:T(128)}, f32[9,256,256]{2,1,0:T(8,128)}, s32[9]{0:T(128)S(1)}, bf16[2,9,32,288]{3,2,1,0:T(8,128)(2,1)}, bf16[256,288,4,4]{0,2,3,1:T(4,128)(2...) while((s32[]{:T(128)}, f32[9,256,256]{2,1,0:T(8,128)}, ...), condition=%wide.region_4.6_spmd, body=%wide.region_3.5_spmd.sunk | while | flops 625213440 | bytes 27392680 | solution.py:73
  360.7 6.4 fusion.55
  367.1 5.0 reshape.87
  383.7 6.4 fusion.55
  390.1 5.0 reshape.87
  406.7 6.4 fusion.55
  413.1 5.0 reshape.87
  429.7 6.4 fusion.55
  452.6 6.4 fusion.55
  475.6 6.4 fusion.55
  498.5 6.4 fusion.55
  521.4 6.4 fusion.55
  544.4 6.4 fusion.55
  559.9 80.2 %reduce-scatter.5.cloned.1.call-done = f32[9,8,256]{2,1,0:T(8,128)} async-done(((f32[9,256,256]{2,1,0:T(8,128)}), f32[9,8,256]{2,1,0:T(8,128)}) %reduce-scatter.5.cloned.1.call-update) | async-done | bytes 73744 | tf_op jit(solution)/shard_map/reduce_scatter | solution.py:74
  (229 shorter events, 274.2 us)
Async XLA Ops:
  6.5 553.3 %reduce-scatter.3.cloned.1.call-start = ((), (), s32[]{:S(2)}) async-start(), calls=%async_computation.3 | async-start | bytes 2433024 | tf_op jit(solution)/shard_map/reduce_scatter | solution.py:74
  51.4 3.0 copy-start.2
  53.8 26.2 %collective-permute-start = (bf16[256,3,1536]{2,0,1:T(8,128)(2,1)S(1)}, bf16[256,3,1536]{2,0,1:T(8,128)(2,1)}, u32[]{:S(2)}, u32[]{:S(2)}) collective-permute-start(bf16[256,3,1536]{2,0,1:T(8,128)(2,1)S(1)} %copy.36), channel_id=1, source_target_pairs={{0,1},{1,2},{2,3},{3,4},{4,5},{5,6},{6,7},{7,8},{8,9},{9,10},{10,1... | collective-permute-start | bytes 7077896 | tf_op jit(solution)/shard_map/ppermute | solution.py:19
  54.2 29.5 %collective-permute-start.1 = (bf16[256,3,1536]{2,0,1:T(8,128)(2,1)S(1)}, bf16[256,3,1536]{2,0,1:T(8,128)(2,1)}, u32[]{:S(2)}, u32[]{:S(2)}) collective-permute-start(bf16[256,3,1536]{2,0,1:T(8,128)(2,1)S(1)} %copy.36), channel_id=1, source_target_pairs={{1,0},{2,1},{3,2},{4,3},{5,4},{6,5},{7,6},{8,7},{9,8},{10,9},{11,1... | collective-permute-start | bytes 7077896 | tf_op jit(solution)/shard_map/ppermute | solution.py:21
  83.6 3.9 copy-start
  122.7 4.5 copy-start.1
  338.0 302.0 %reduce-scatter.5.cloned.1.call-start = ((), (), s32[]{:S(2)}) async-start(), calls=%async_computation.4 | async-start | bytes 2433024 | tf_op jit(solution)/shard_map/reduce_scatter | solution.py:74
Sparse Core Ops, SparseCore 0:
  338.1 80.0 reduce-scatter.2
  560.0 80.0 reduce-scatter.4
where the time goes:
time: 653 us; the launch traced here: 648 us
  matrix products  236 us (36%)
  local copies, waits for them, and re-layouts  197 us (30%)
  waiting for transfers between devices  106 us (16%)
  blocking collectives  40.8 us (6%)
  loops' own time  37.9 us (6%)
  other arithmetic  16.7 us (3%)
  between operations  13.5 us (2%)
    dot_general x18, matrix products, make_diff(): jnp.einsum('dck,skvc->skvd', g_cond, own, preferred_element_type=jnp.floa...  115 us
    reshape x18, local copies, waits for them, and re-layouts, make_diff(): return (elec - hole).astype(jnp.bfloat16).reshape(states, local_k * 16)  89.7 us
    reduce_scatter x2, waiting for transfers between devices, shards(): lax.psum_scatter(partial_sum, 'ka', scatter_dimension=1, tiled=True)  80.2 us
    dot_general x18, matrix products, make_diff(): jnp.einsum('vwk,skvc->skwc', g_val, own, preferred_element_type=jnp.float32)  62.9 us
    dot_general x18, matrix products, per_mode(): jnp.einsum('ap,bp->ab', left_rows, diff, preferred_element_type=jnp.float32)  57.6 us
    all_to_all x1, blocking collectives, shards(): mine = lax.all_to_all(blocks, 'ka', split_axis=1, concat_axis=0, tiled=True)  40.8 us
    another operation x2, loops' own time, shards(): partial_sum = lax.map(per_mode, jnp.arange(NU, dtype=jnp.int32))  37.9 us
    ppermute x1, waiting for transfers between devices, extended(): lax.ppermute(tail, axis, [(i, (i + 1) % count) for i in range(count)])  25.5 us
  transfers between devices with their start and end apart: 4, of which 2 were waited for; matrix products, arithmetic and copies ran while one was open for 32% of the time, Pallas kernels for 0%

commit v1 on v0

v1 whole, which is shorter than its diff:
```python
import math

import jax
import jax.numpy as jnp
from jax import lax
from jax.experimental import pallas as pl
from jax.experimental.pallas import tpu as pltpu
from jax.sharding import PartitionSpec as P

BF = jnp.bfloat16
F32 = jnp.float32
NU = 9
KY = 96
L = KY * 16
CHIPS = 16
ROWS = 8
S = CHIPS * 2 * ROWS
HALF = 288
QUART = L // 4
MESH = pl.DeviceIdType.MESH
NT = (((1,), (1,)), ((), ()))


def build_coefficients(cs, u, lo, h):
    c = cs[h].reshape(NU * 32, HALF)
    kk = lax.broadcasted_iota(jnp.int32, (HALF, L), 0)
    col = lax.broadcasted_iota(jnp.int32, (HALF, L), 1) // 16
    j = lax.broadcasted_iota(jnp.int32, (32, L), 0)
    band = lax.broadcasted_iota(jnp.int32, (32, L), 1) % 16
    keep = jnp.where(j < 16, (j // 4) - band % 4, (j % 4) - band // 4) == 0
    si = lax.broadcasted_iota(jnp.int32, (32, 32), 0)
    sj = lax.broadcasted_iota(jnp.int32, (32, 32), 1)
    picks = jnp.where(
        si < 16,
        jnp.where(sj < 16, jnp.where(sj % 4 == si % 4, 1.0, 0.0), 0.0),
        jnp.where(sj >= 16, jnp.where(sj // 4 == si // 4, 1.0, 0.0), 0.0),
    ).astype(BF)
    i16 = lax.broadcasted_iota(jnp.int32, (16, L), 0)
    b16 = lax.broadcasted_iota(jnp.int32, (16, L), 1) % 16
    same_v = (b16 // 4) == (i16 // 4)
    same_c = (b16 % 4) == (i16 % 4)

    def line(l3, carry):
        spread = (kk == (KY * l3 + col)).astype(F32).astype(BF)
        wide = jnp.dot(c, spread, preferred_element_type=F32)
        for nu in range(NU):
            kept = jnp.where(keep, wide[nu * 32 : (nu + 1) * 32], 0.0).astype(BF)
            w = jnp.dot(picks, kept, preferred_element_type=F32)
            full = jnp.where(same_v, w[:16], 0.0) - jnp.where(same_c, w[16:], 0.0)
            high = full.astype(BF)
            u[3 * h + l3, nu] = high
            lo[3 * h + l3, nu : nu + 1, :] = jnp.sum(full - high.astype(F32), axis=0, keepdims=True)
        return carry

    lax.fori_loop(0, 3, line, 0)


def diff_line(win, u, lo, d, line):
    rk = lax.broadcasted_iota(jnp.int32, (256, 256), 0) // 16
    ck = lax.broadcasted_iota(jnp.int32, (256, 256), 1) // 16
    block = rk == ck
    start = pl.multiple_of(line * L, 128)

    def mode(nu, carry):
        for t in range(L // 256):
            ts = slice(t * 256, (t + 1) * 256)
            a = win[3 + line, :, :, :, ts].reshape(S, 256)
            m = jnp.where(block, jnp.tile(u[line, nu, :, ts], (16, 1)), jnp.zeros((), BF))
            x = jnp.dot(a, m, preferred_element_type=F32)
            x = x + lo[line, pl.ds(nu, 1), ts] * a.astype(F32)
            d[nu, :, pl.ds(start + t * 256, 256)] = x.astype(BF)
        return carry

    lax.fori_loop(0, NU, mode, 0)


def kernel(
    move, env, coupling, out,
    win, cs, u, lo, d, sh, gs, rb,
    loc, s_coup, r_coup, s_halo, r_halo, s_own, r_own,
    s_rel, r_rel, s_relh, r_relh, s_y, r_y, s_red, r_red,
):
    y = lax.axis_index("pb")
    r = lax.axis_index("ka")
    chip, i = r // 2, r % 2
    up, down = (y + 1) % 4, (y + 3) % 4
    sib = (y, r + 1 - 2 * i)
    quarter = pl.ds(pl.multiple_of(y * QUART, 128), QUART)

    def remote(src, dst, ss, rs, dev):
        return pltpu.make_async_remote_copy(
            src_ref=src, dst_ref=dst, send_sem=ss, recv_sem=rs, device_id=dev, device_id_type=MESH
        )

    def drain(ref, sem):
        pltpu.make_async_copy(ref, ref, sem).wait()

    barrier = pltpu.get_barrier_semaphore()

    def greet(k, carry):
        pl.semaphore_signal(barrier, inc=1, device_id=(y, (r + k) % 32), device_id_type=MESH)
        return carry

    lax.fori_loop(1, 32, greet, 0)
    for other in (up, down):
        pl.semaphore_signal(barrier, inc=1, device_id=(other, r), device_id_type=MESH)
    pl.semaphore_wait(barrier, 33)

    other_q = remote(coupling.at[1 - i], cs.at[i], s_coup, r_coup, sib)
    other_q.start()
    mine_q = pltpu.make_async_copy(coupling.at[i], cs.at[i], loc.at[0])
    mine_q.start()

    left, right = pl.ds(0, 3), pl.ds(9, 3)

    def send_halo(k, carry):
        t = (chip + k) % CHIPS
        dev = (y, 2 * t + i)
        before, after = (2 * t + 31) % 32, (2 * t + 2) % 32
        remote(env.at[pl.ds(3 * before, 3), :, quarter], win.at[left, chip, i, :, quarter], s_halo, r_halo, dev).start()
        remote(env.at[pl.ds(3 * after, 3), :, quarter], win.at[right, chip, i, :, quarter], s_halo, r_halo, dev).start()
        return carry

    lax.fori_loop(1, CHIPS, send_halo, 0)
    before, after = (2 * chip + 31) % 32, (2 * chip + 2) % 32
    own_left = pltpu.make_async_copy(env.at[pl.ds(3 * before, 3), :, quarter], win.at[left, chip, i, :, quarter], loc.at[1])
    own_right = pltpu.make_async_copy(env.at[pl.ds(3 * after, 3), :, quarter], win.at[right, chip, i, :, quarter], loc.at[2])
    own_mid = pltpu.make_async_copy(env.at[pl.ds(6 * chip, 6)], win.at[pl.ds(3, 6), chip, i], loc.at[3])
    own_left.start()
    own_right.start()
    own_mid.start()

    def send_line(l, carry):
        def to(k, carry):
            t = (chip + k) % CHIPS
            remote(env.at[6 * t + l], win.at[3 + l, chip, i], s_own.at[l], r_own.at[l], (y, 2 * t + i)).start()
            return carry

        return lax.fori_loop(1, CHIPS, to, carry)

    lax.fori_loop(0, 6, send_line, 0)

    mine_q.wait()
    build_coefficients(cs, u, lo, i)

    own_left.wait()
    own_right.wait()
    own_mid.wait()
    drain(win.at[pl.ds(0, 6), pl.ds(0, CHIPS - 1), i, :, pl.ds(0, QUART)], r_halo)

    def part(lines, q):
        return win.at[lines, :, i, :, pl.ds(pl.multiple_of(q * QUART, 128), QUART)]

    def hand(n, lines, q, dev, sem):
        piece = part(lines, q)
        copy = remote(piece, piece, s_y.at[n], r_y.at[n], dev)
        copy.start()
        return copy

    def relay_halo(lines, q):
        piece = part(lines, q)
        remote(piece, piece, s_relh, r_relh, sib).start()

    step1 = [
        hand(0, left, y, (up, r), None),
        hand(1, right, y, (down, r), None),
        hand(2, right, y, (up, r), None),
        hand(3, left, y, (down, r), None),
    ]
    relay_halo(left, y)
    relay_halo(right, y)

    other_q.wait()
    build_coefficients(cs, u, lo, 1 - i)

    def relay_line(l):
        drain(win.at[3 + l, pl.ds(0, CHIPS - 1), i], r_own.at[l])
        piece = win.at[3 + l, :, i]
        remote(piece, piece, s_rel.at[l], r_rel.at[l], sib).start()

    def line_ready(l):
        drain(win.at[3 + l, :, 1 - i], r_rel.at[l])

    relay_line(0)
    step1[0].wait()
    step1[1].wait()
    step2 = [hand(4, left, down, (up, r), None), hand(5, right, up, (down, r), None)]
    relay_halo(left, down)
    relay_halo(right, up)
    step1[2].wait()
    step1[3].wait()
    relay_halo(right, down)
    relay_halo(left, up)

    for l in range(6):
        if l < 5:
            relay_line(l + 1)
        line_ready(l)
        diff_line(win, u, lo, d, l)
        if l == 3:
            step2[0].wait()
            step2[1].wait()
            far = (y + 2) % 4
            relay_halo(left, far)
            relay_halo(right, far)

    drain(win.at[pl.ds(0, 6), :, 1 - i], r_relh)

    first, turn = move[0], move[1]

    def shift(l, carry):
        x = win[l + first].reshape(S, L)
        sh[:, pl.ds(pl.multiple_of(l * L, 128), L)] = pltpu.roll(x.astype(F32), turn, 1).astype(BF)
        return carry

    lax.fori_loop(0, 6, shift, 0)

    def mode(nu, carry):
        g = lax.dot_general(sh[...], d[nu], NT, preferred_element_type=F32)
        gs[nu] = g.astype(BF).reshape(2 * CHIPS, ROWS, S)

        def to(k, carry):
            o = (r + k) % 32
            remote(gs.at[nu, o], rb.at[nu, r], s_red, r_red, (y, o)).start()
            return carry

        return lax.fori_loop(1, 32, to, carry)

    lax.fori_loop(0, NU, mode, 0)
    keep_own = pltpu.make_async_copy(gs.at[:, r], rb.at[:, r], loc.at[4])
    keep_own.start()

    drain(win.at[pl.ds(0, 6), pl.ds(0, CHIPS - 1), i, :, pl.ds(0, QUART)], s_halo)
    for l in range(6):
        drain(win.at[3 + l, pl.ds(0, CHIPS - 1), i], s_own.at[l])
        drain(win.at[3 + l, :, i], s_rel.at[l])
    drain(win.at[pl.ds(0, 6), :, i], s_relh)
    keep_own.wait()
    drain(gs.at[:, pl.ds(0, 31)], s_red)
    drain(rb.at[:, pl.ds(0, 31)], r_red)

    factor = 1.0 / math.sqrt(16.0 * CHIPS * 2 * HALF)

    def total(nu, carry):
        for q in range(2):
            acc = rb[nu, q].astype(F32)
            for c in range(1, CHIPS):
                acc = acc + rb[nu, 2 * c + q].astype(F32)
            out[q, nu] = acc * factor
        return carry

    lax.fori_loop(0, NU, total, 0)


def shards(envelopes, coupling, kq_map):
    r = lax.axis_index("ka")
    mine = lax.dynamic_index_in_dim(kq_map[:, 0], r % 2, 0, keepdims=False)
    step_x = (mine // KY - 3 * r + 3 + 2 * KY) % KY
    turn = (L - 16 * (mine % KY)) % L
    move = jnp.stack([step_x, turn]).astype(jnp.int32)
    env = envelopes.reshape(ROWS, KY, L).transpose(1, 0, 2)
    dma = pltpu.SemaphoreType.DMA
    return pl.pallas_call(
        kernel,
        out_shape=jax.ShapeDtypeStruct((2, NU, ROWS, S), F32),
        in_specs=[
            pl.BlockSpec(memory_space=pltpu.SMEM),
            pl.BlockSpec(memory_space=pl.ANY),
            pl.BlockSpec(memory_space=pl.ANY),
        ],
        out_specs=pl.BlockSpec(memory_space=pltpu.VMEM),
        scratch_shapes=[
            pltpu.VMEM((12, CHIPS, 2, ROWS, L), BF),
            pltpu.VMEM((2, NU, 32, HALF), BF),
            pltpu.VMEM((6, NU, 16, L), BF),
            pltpu.VMEM((6, 16, L), F32),
            pltpu.VMEM((NU, S, 6 * L), BF),
            pltpu.VMEM((S, 6 * L), BF),
            pltpu.VMEM((NU, 32, ROWS, S), BF),
            pltpu.VMEM((NU, 32, ROWS, S), BF),
            dma((5,)), dma, dma, dma, dma, dma((6,)), dma((6,)),
            dma((6,)), dma((6,)), dma, dma, dma((6,)), dma((6,)), dma, dma,
        ],
        compiler_params=pltpu.CompilerParams(
            collective_id=0, has_side_effects=True, vmem_limit_bytes=67043328
        ),
        name="exciton_coupling",
    )(move, env, coupling)


def solution(mesh):
    return jax.shard_map(
        shards,
        mesh=mesh,
        in_specs=(P("ka", None), P("pb", None, None, "ka"), P("pb", "ka")),
        out_specs=P("pb", None, "ka", None),
        check_vma=False,
    )
```

time: 653 us -> 90.8 us (0.14)
  matrix products: 236 us -> 0 us
  local copies, waits for them, and re-layouts: 197 us -> 2.26 us
  waiting for transfers between devices: 106 us -> 0 us
  Pallas kernels: 0 us -> 83.3 us
  blocking collectives: 40.8 us -> 0 us
  loops' own time: 37.9 us -> 0 us
  other arithmetic: 16.7 us -> 1.18 us
  between operations: 13.5 us -> 3.92 us
    dot_general x54 -> x0, matrix products: 236 us -> none  [the longest x18 115 us: make_diff(): jnp.einsum('dck,skvc->skvd', g_cond, own, preferred_element_type=jnp.floa...]
    reshape x92 -> x0, local copies, waits for them, and re-layouts: 105 us -> none  [the longest x18 89.7 us: make_diff(): return (elec - hole).astype(jnp.bfloat16).reshape(states, local_k * 16)]
    pallas_call x0 -> x1, Pallas kernels: none -> 83.3 us  [shards(): pl.pallas_call(kernel, out_shape=jax.ShapeDtypeStruct((2, NU, ROWS, S), F...]
    reduce_scatter x2 -> x0, waiting for transfers between devices: 80.2 us -> none  [shards(): lax.psum_scatter(partial_sum, 'ka', scatter_dimension=1, tiled=True)]
    all_to_all x1 -> x0, blocking collectives: 40.8 us -> none  [shards(): mine = lax.all_to_all(blocks, 'ka', split_axis=1, concat_axis=0, tiled=True)]
    another operation x2 -> x0, loops' own time: 37.9 us -> none  [shards(): partial_sum = lax.map(per_mode, jnp.arange(NU, dtype=jnp.int32))]
    ppermute x2 -> x0, waiting for transfers between devices: 25.5 us -> none  [the longest x1 25.5 us: extended(): lax.ppermute(tail, axis, [(i, (i + 1) % count) for i in range(count)])]
    slice x21 -> x1, local copies, waits for them, and re-layouts: 17.3 us -> 0.68 us  [shards(): mine = lax.dynamic_index_in_dim(kq_map[:, 0], r % 2, 0, keepdims=False)]
  transfers between devices with their start and end apart: 4 -> 0, of which waited for: 2 -> 0; matrix products, arithmetic and copies ran while one was open for 32% -> 0% of each run, Pallas kernels for 0% -> 0%
where the time goes in v1:
time: 90.8 us; the launch traced here: 90.6 us
  Pallas kernels  83.3 us (92%)
  between operations  3.92 us (4%)
  local copies, waits for them, and re-layouts  2.26 us (2%)
  other arithmetic  1.18 us (1%)
    pallas_call x1, Pallas kernels, shards(): pl.pallas_call(kernel, out_shape=jax.ShapeDtypeStruct((2, NU, ROWS, S), F...  83.3 us

profile of v1, /device:TPU:1, one launch (start us, length us, event | category | flops | bytes accessed | tf_op | source)
XLA Modules:
  0.0 90.6 jit_solution(4672834950513892649)
XLA Ops:
  0.0 0.7 slice.3
  0.7 0.5 fusion
  5.1 0.6 pad_add_fusion.move
  5.8 83.3 %exciton_coupling.1 = f32[2,9,8,256]{3,2,1,0:T(8,128)} custom-call(s32[2]{0:T(128)} %pad_add_fusion.move, bf16[96,8,1536]{2,1,0:T(8,128)(2,1)} %bitcast.8, bf16[2,9,32,288]{3,2,1,0:T(8,128)(2,1)} %coupling.1), custom_call_target="tpu_custom_call" | custom-call | tf_op jit(solution)/shard_map/exciton_coupling/pallas_call | solution.py:263
  89.0 1.6 %copy.5 = f32[2,9,8,256]{3,2,1,0:T(8,128)} copy(f32[2,9,8,256]{3,2,1,0:T(8,128)} %exciton_coupling.1) | data formatting | bytes 294912

commit v2 on v1

v2 whole, which is shorter than its diff:
```python
import math

import jax
import jax.numpy as jnp
from jax import lax
from jax.experimental import pallas as pl
from jax.experimental.pallas import tpu as pltpu
from jax.sharding import PartitionSpec as P

BF = jnp.bfloat16
F32 = jnp.float32
NU = 9
KY = 96
L = KY * 16
CHIPS = 16
ROWS = 8
S = CHIPS * 2 * ROWS
HALF = 288
QUART = L // 4
MESH = pl.DeviceIdType.MESH
NT = (((1,), (1,)), ((), ()))


def build_coefficients(cs, u, lo, h):
    c = cs[h].reshape(NU * 32, HALF)
    kk = lax.broadcasted_iota(jnp.int32, (HALF, L), 0)
    col = lax.broadcasted_iota(jnp.int32, (HALF, L), 1) // 16
    j = lax.broadcasted_iota(jnp.int32, (32, L), 0)
    band = lax.broadcasted_iota(jnp.int32, (32, L), 1) % 16
    keep = jnp.where(j < 16, (j // 4) - band % 4, (j % 4) - band // 4) == 0
    si = lax.broadcasted_iota(jnp.int32, (32, 32), 0)
    sj = lax.broadcasted_iota(jnp.int32, (32, 32), 1)
    picks = jnp.where(
        si < 16,
        jnp.where(sj < 16, jnp.where(sj % 4 == si % 4, 1.0, 0.0), 0.0),
        jnp.where(sj >= 16, jnp.where(sj // 4 == si // 4, 1.0, 0.0), 0.0),
    ).astype(BF)
    i16 = lax.broadcasted_iota(jnp.int32, (16, L), 0)
    b16 = lax.broadcasted_iota(jnp.int32, (16, L), 1) % 16
    same_v = (b16 // 4) == (i16 // 4)
    same_c = (b16 % 4) == (i16 % 4)

    def line(l3, carry):
        spread = (kk == (KY * l3 + col)).astype(F32).astype(BF)
        wide = jnp.dot(c, spread, preferred_element_type=F32)
        for nu in range(NU):
            kept = jnp.where(keep, wide[nu * 32 : (nu + 1) * 32], 0.0).astype(BF)
            w = jnp.dot(picks, kept, preferred_element_type=F32)
            full = jnp.where(same_v, w[:16], 0.0) - jnp.where(same_c, w[16:], 0.0)
            high = full.astype(BF)
            u[3 * h + l3, nu] = high
            lo[3 * h + l3, nu : nu + 1, :] = jnp.sum(full - high.astype(F32), axis=0, keepdims=True)
        return carry

    lax.fori_loop(0, 3, line, 0)


def diff_line(win, u, lo, d, line):
    rk = lax.broadcasted_iota(jnp.int32, (256, 256), 0) // 16
    ck = lax.broadcasted_iota(jnp.int32, (256, 256), 1) // 16
    block = rk == ck
    start = pl.multiple_of(line * L, 128)

    def mode(nu, carry):
        for t in range(L // 256):
            ts = slice(t * 256, (t + 1) * 256)
            a = win[3 + line, :, :, :, ts].reshape(S, 256)
            m = jnp.where(block, jnp.tile(u[line, nu, :, ts], (16, 1)), jnp.zeros((), BF))
            x = jnp.dot(a, m, preferred_element_type=F32)
            x = x + lo[line, pl.ds(nu, 1), ts] * a.astype(F32)
            d[nu, :, pl.ds(start + t * 256, 256)] = x.astype(BF)
        return carry

    lax.fori_loop(0, NU, mode, 0)


def kernel(
    kq, env, coupling, out,
    win, cs, u, lo, d, sh, gs, rb,
    loc, s_coup, r_coup, s_q, r_q, s_dir, r_dir,
    s_rel, r_rel, s_relq, r_relq, s_y, r_y, s_red, r_red,
):
    y = lax.axis_index("pb")
    r = lax.axis_index("ka")
    chip, i = r // 2, r % 2
    up, down, far = (y + 1) % 4, (y + 3) % 4, (y + 2) % 4
    sib = (y, r + 1 - 2 * i)

    def quarter(q):
        return pl.ds(pl.multiple_of(q * QUART, 128), QUART)

    def remote(src, dst, ss, rs, dev):
        return pltpu.make_async_remote_copy(
            src_ref=src, dst_ref=dst, send_sem=ss, recv_sem=rs, device_id=dev, device_id_type=MESH
        )

    def drain(ref, sem):
        pltpu.make_async_copy(ref, ref, sem).wait()

    barrier = pltpu.get_barrier_semaphore()

    def greet(k, carry):
        pl.semaphore_signal(barrier, inc=1, device_id=(y, (r + k) % 32), device_id_type=MESH)
        return carry

    lax.fori_loop(1, 32, greet, 0)
    for other in (up, down):
        pl.semaphore_signal(barrier, inc=1, device_id=(other, r), device_id_type=MESH)
    pl.semaphore_wait(barrier, 33)

    spans = (pl.ds(6, 3), pl.ds(0, 3), pl.ds(9, 3))

    def source(g, t):
        block = ((2 * t + 1) % 32, (2 * t + 31) % 32, (2 * t + 2) % 32)[g]
        return env.at[pl.ds(3 * block, 3), :, quarter(y)]

    def send_group(g):
        def to(k, carry):
            t = (chip + k) % CHIPS
            remote(
                source(g, t), win.at[spans[g], chip, i, :, quarter(y)], s_q.at[g], r_q.at[g], (y, 2 * t + i)
            ).start()
            return carry

        lax.fori_loop(1, CHIPS, to, 0)

    def send_line(l):
        def to(k, carry):
            t = (chip + k) % CHIPS
            remote(env.at[6 * t + l], win.at[3 + l, chip, i], s_dir.at[l], r_dir.at[l], (y, 2 * t + i)).start()
            return carry

        lax.fori_loop(1, CHIPS, to, 0)

    send_group(0)
    other_q = remote(coupling.at[1 - i], cs.at[i], s_coup, r_coup, sib)
    other_q.start()
    mine_q = pltpu.make_async_copy(coupling.at[i], cs.at[i], loc.at[0])
    mine_q.start()
    kept = [
        pltpu.make_async_copy(source(g, chip), win.at[spans[g], chip, i, :, quarter(y)], loc.at[1 + g])
        for g in range(3)
    ]
    kept.append(pltpu.make_async_copy(env.at[pl.ds(6 * chip, 3)], win.at[pl.ds(3, 3), chip, i], loc.at[4]))
    for copy in kept:
        copy.start()
    send_line(0)
    send_group(1)
    send_group(2)
    send_line(1)
    send_line(2)

    def arrived(g):
        drain(win.at[pl.ds(0, 3), pl.ds(0, CHIPS - 1), i, :, quarter(0)], r_q.at[g])

    def relay(g, q):
        piece = win.at[spans[g], :, i, :, quarter(q)]
        remote(piece, piece, s_relq.at[g], r_relq.at[g], sib).start()

    def along(g, n, q, chips, dev):
        piece = win.at[spans[g], chips, i, :, quarter(q)]
        copy = remote(piece, piece, s_y.at[4 * g + n], r_y.at[4 * g + n], (dev, r))
        copy.start()
        return copy

    def first_step(g):
        arrived(g)
        every = pl.ds(0, CHIPS)
        copies = [along(g, 0, y, every, up), along(g, 1, y, every, down)]
        relay(g, y)
        return copies

    def second_step(g, copies):
        copies[0].wait()
        copies[1].wait()
        half = CHIPS // 2
        copies = [along(g, 2, down, pl.ds(0, half), up), along(g, 3, up, pl.ds(half, half), down)]
        relay(g, down)
        relay(g, up)
        return copies

    def last_step(g, copies):
        copies[0].wait()
        copies[1].wait()
        relay(g, far)

    def group_ready(g):
        drain(win.at[pl.ds(0, 3), :, 1 - i], r_relq.at[g])

    def relay_line(l):
        drain(win.at[3 + l, pl.ds(0, CHIPS - 1), i], r_dir.at[l])
        piece = win.at[3 + l, :, i]
        remote(piece, piece, s_rel.at[l], r_rel.at[l], sib).start()

    def line_ready(l):
        drain(win.at[3 + l, :, 1 - i], r_rel.at[l])

    def diff(l):
        diff_line(win, u, lo, d, l)

    for copy in kept:
        copy.wait()
    own1 = first_step(0)
    mine_q.wait()
    build_coefficients(cs, u, lo, i)
    other_q.wait()
    build_coefficients(cs, u, lo, 1 - i)
    relay_line(0)
    own2 = second_step(0, own1)
    line_ready(0)
    diff(0)
    before1 = first_step(1)
    last_step(0, own2)
    group_ready(0)
    diff(3)
    after1 = first_step(2)
    diff(4)
    before2 = second_step(1, before1)
    relay_line(1)
    diff(5)
    after2 = second_step(2, after1)
    line_ready(1)
    diff(1)
    relay_line(2)
    last_step(1, before2)
    line_ready(2)
    diff(2)
    last_step(2, after2)
    group_ready(1)
    group_ready(2)

    target = kq[i, 0]
    first = jnp.minimum((target // KY - 3 * r + 3 + 2 * KY) % KY, 6)
    turn = (L - 16 * (target % KY)) % L

    def shift(l, carry):
        for n in range(4):
            x = win[l + first, 4 * n : 4 * n + 4].reshape(64, L)
            x = pltpu.roll(x.astype(F32), turn, 1).astype(BF)
            sh[64 * n : 64 * n + 64, pl.ds(pl.multiple_of(l * L, 128), L)] = x
        return carry

    lax.fori_loop(0, 6, shift, 0)

    def partial_sum(nu):
        g = lax.dot_general(sh[...], d[nu], NT, preferred_element_type=F32)
        gs[nu] = g.astype(BF).reshape(2 * CHIPS, ROWS, S)

    def send_sum(nu):
        for k in range(1, 32):
            o = (r + k) % 32
            remote(gs.at[nu, o], rb.at[nu, r], s_red, r_red.at[nu], (y, o)).start()

    def mode(nu, carry):
        send_sum(nu - 1)
        partial_sum(nu)
        return carry

    partial_sum(0)
    lax.fori_loop(1, NU, mode, 0)
    keep_own = pltpu.make_async_copy(gs.at[:, r], rb.at[:, r], loc.at[5])
    keep_own.start()

    for g in range(3):
        drain(win.at[pl.ds(0, 3), pl.ds(0, CHIPS - 1), i, :, quarter(0)], s_q.at[g])
        drain(win.at[pl.ds(0, 3), :, i], s_relq.at[g])
        drain(win.at[3 + g, pl.ds(0, CHIPS - 1), i], s_dir.at[g])
        drain(win.at[3 + g, :, i], s_rel.at[g])
    keep_own.wait()
    send_sum(NU - 1)

    factor = 1.0 / math.sqrt(16.0 * CHIPS * 2 * HALF)

    def total(nu, carry):
        drain(rb.at[nu, pl.ds(0, 31)], r_red.at[nu])
        for q in range(2):
            acc = rb[nu, q].astype(F32)
            for c in range(1, CHIPS):
                acc = acc + rb[nu, 2 * c + q].astype(F32)
            out[q, nu] = acc * factor
        return carry

    lax.fori_loop(0, NU, total, 0)
    drain(gs.at[:, pl.ds(0, 31)], s_red)


def shards(envelopes, coupling, kq_map):
    env = envelopes.reshape(ROWS, KY, L).transpose(1, 0, 2)
    dma = pltpu.SemaphoreType.DMA
    return pl.pallas_call(
        kernel,
        out_shape=jax.ShapeDtypeStruct((2, NU, ROWS, S), F32),
        in_specs=[
            pl.BlockSpec(memory_space=pltpu.SMEM),
            pl.BlockSpec(memory_space=pl.ANY),
            pl.BlockSpec(memory_space=pl.ANY),
        ],
        out_specs=pl.BlockSpec(memory_space=pltpu.VMEM),
        scratch_shapes=[
            pltpu.VMEM((12, CHIPS, 2, ROWS, L), BF),
            pltpu.VMEM((2, NU, 32, HALF), BF),
            pltpu.VMEM((6, NU, 16, L), BF),
            pltpu.VMEM((6, 16, L), F32),
            pltpu.VMEM((NU, S, 6 * L), BF),
            pltpu.VMEM((S, 6 * L), BF),
            pltpu.VMEM((NU, 32, ROWS, S), BF),
            pltpu.VMEM((NU, 32, ROWS, S), BF),
            dma((6,)), dma, dma, dma((3,)), dma((3,)), dma((3,)), dma((3,)),
            dma((3,)), dma((3,)), dma((3,)), dma((3,)), dma((12,)), dma((12,)), dma, dma((NU,)),
        ],
        compiler_params=pltpu.CompilerParams(
            collective_id=0, has_side_effects=True, vmem_limit_bytes=67043328
        ),
        name="exciton_coupling",
    )(kq_map, env, coupling)


def solution(mesh):
    return jax.shard_map(
        shards,
        mesh=mesh,
        in_specs=(P("ka", None), P("pb", None, None, "ka"), P("pb", "ka")),
        out_specs=P("pb", None, "ka", None),
        check_vma=False,
    )
```

time: 90.8 us -> 79.3 us (0.87)
  Pallas kernels: 83.3 us -> 77.6 us
  between operations: 3.92 us -> 0.01 us
  other arithmetic: 1.18 us -> 0 us
    pallas_call x1, Pallas kernels: 83.3 us -> 77.6 us  [shards(): pl.pallas_call(kernel, out_shape=jax.ShapeDtypeStruct((2, NU, ROWS, S), F...]
where the time goes in v2:
time: 79.3 us; the launch traced here: 79.2 us
  Pallas kernels  77.6 us (98%)
  local copies, waits for them, and re-layouts  1.58 us (2%)
    pallas_call x1, Pallas kernels, shards(): pl.pallas_call(kernel, out_shape=jax.ShapeDtypeStruct((2, NU, ROWS, S), F...  77.6 us

profile of v2, /device:TPU:1, one launch (start us, length us, event | category | flops | bytes accessed | tf_op | source)
XLA Modules:
  0.0 79.2 jit_solution(16614900440326898216)
XLA Ops:
  0.0 77.6 %exciton_coupling.1 = f32[2,9,8,256]{3,2,1,0:T(8,128)} custom-call(s32[2,288]{1,0:T(2,128)} %kq.1, bf16[96,8,1536]{2,1,0:T(8,128)(2,1)} %bitcast.3, bf16[2,9,32,288]{3,2,1,0:T(8,128)(2,1)} %coupling.1), custom_call_target="tpu_custom_call" | custom-call | tf_op jit(solution)/shard_map/exciton_coupling/pallas_call | solution.py:290
  77.6 1.6 %copy.5 = f32[2,9,8,256]{3,2,1,0:T(8,128)} copy(f32[2,9,8,256]{3,2,1,0:T(8,128)} %exciton_coupling.1) | data formatting | bytes 294912

commit v3 on v2

--- a/solution.py
+++ b/solution.py
@@ -61,17 +61,26 @@
     block = rk == ck
     start = pl.multiple_of(line * L, 128)
 
-    def mode(nu, carry):
+    def modes(n, carry):
         for t in range(L // 256):
             ts = slice(t * 256, (t + 1) * 256)
             a = win[3 + line, :, :, :, ts].reshape(S, 256)
-            m = jnp.where(block, jnp.tile(u[line, nu, :, ts], (16, 1)), jnp.zeros((), BF))
-            x = jnp.dot(a, m, preferred_element_type=F32)
-            x = x + lo[line, pl.ds(nu, 1), ts] * a.astype(F32)
-            d[nu, :, pl.ds(start + t * 256, 256)] = x.astype(BF)
-        return carry
-
-    lax.fori_loop(0, NU, mode, 0)
+            wide = jnp.concatenate(
+                [
+                    jnp.where(block, jnp.tile(u[line, 3 * n + m, :, ts], (16, 1)), jnp.zeros((), BF))
+                    for m in range(3)
+                ],
+                axis=1,
+            )
+            x = jnp.dot(a, wide, preferred_element_type=F32)
+            af = a.astype(F32)
+            for m in range(3):
+                nu = 3 * n + m
+                piece = x[:, 256 * m : 256 * m + 256] + lo[line, pl.ds(nu, 1), ts] * af
+                d[nu, :, pl.ds(start + t * 256, 256)] = piece.astype(BF)
+        return carry
+
+    lax.fori_loop(0, NU // 3, modes, 0)
 
 
 def kernel(

time: 79.3 us -> 76.9 us (0.970)
  Pallas kernels: 77.6 us -> 75.2 us
    pallas_call x1, Pallas kernels: 77.6 us -> 75.2 us  [shards(): pl.pallas_call(kernel, out_shape=jax.ShapeDtypeStruct((2, NU, ROWS, S), F...]
where the time goes in v3:
time: 76.9 us; the launch traced here: 76.8 us
  Pallas kernels  75.2 us (98%)
  local copies, waits for them, and re-layouts  1.58 us (2%)
    pallas_call x1, Pallas kernels, shards(): pl.pallas_call(kernel, out_shape=jax.ShapeDtypeStruct((2, NU, ROWS, S), F...  75.2 us
    unnamed x1, local copies, waits for them, and re-layouts  1.58 us

profile of v3, /device:TPU:1, one launch (start us, length us, event | category | flops | bytes accessed | tf_op | source)
XLA Modules:
  0.0 76.8 jit_solution(15575427368409135021)
XLA Ops:
  0.0 75.2 %exciton_coupling.1 = f32[2,9,8,256]{3,2,1,0:T(8,128)} custom-call(s32[2,288]{1,0:T(2,128)} %kq.1, bf16[96,8,1536]{2,1,0:T(8,128)(2,1)} %bitcast.3, bf16[2,9,32,288]{3,2,1,0:T(8,128)(2,1)} %coupling.1), custom_call_target="tpu_custom_call" | custom-call | tf_op jit(solution)/shard_map/exciton_coupling/pallas_call | solution.py:299
  75.2 1.6 %copy.5 = f32[2,9,8,256]{3,2,1,0:T(8,128)} copy(f32[2,9,8,256]{3,2,1,0:T(8,128)} %exciton_coupling.1) | data formatting | bytes 294912
